TPU v7x, 256 devices: a whole 4x4x8 slice. The times are simulated.
256 devices in a mesh: blk: 64 (over z, y, x_lo), feat: 4 (over x_hi, core).
Axes of the slice: x: 4 (x_hi: 2, x_lo: 2; x = x_hi * 2 + x_lo), y: 4, z: 8, core: 2. Of those that a mesh axis runs over, the one named last changes fastest.
Arguments:
- x_t: bfloat16 [256, 262144], P('feat', 'blk'), may hold values from -6 to 6
- weight: bfloat16 [256, 256], P('feat'), may hold values from -0.375 to 0.375
- cotangent: bfloat16 [256, 262144], P('feat', 'blk'), may hold values from -6 to 6
- tile_row: int32 [18432], P('blk'), may hold values from 0 to 31
- tile_col: int32 [18432], P('blk'), may hold values from 0 to 31
- tile_off: int32 [18432], P('blk'), may hold values from -4 to 4, as said below
- tile_vals: bfloat16 [18432, 128, 128], P('blk'), may hold values from -0.625 to 0.625
- tile_count: int32 [64], P('blk'), may hold values from 72 to 288, as said below
Outputs:
- out_t: bfloat16 [256, 262144], P('feat', 'blk')
- grad_x_t: bfloat16 [256, 262144], P('feat', 'blk')
- grad_weight: float32 [256, 256], P('feat')
Inputs may be any that keep to these rules, and one draw needn't show every extreme that they name: `tile_off`: slots 0 to 8 of every partition name each offset once; slots may repeat a tile position, and repeated tiles add. `tile_count`: some partition lists 288 live tiles and some 288 // 4.
All inputs are finite; a program needn't handle non-finite values.
Results may differ from a plain program's by a relative error of at most 0.0062.
Values may be sent and summed in bfloat16 or wider, within the bound.
No kernel may reach another device: no remote copies, remote signals or barrier semaphores. Data moves between devices by JAX's collectives and lax.ppermute only.
A program may use at most 128 MiB of HBM per device.

v0:
```python
import math
import jax
import jax.numpy as jnp
from jax import lax
from jax.sharding import PartitionSpec as P

REACH = 4


def shifted(block, axis, distance):
    devices = range(lax.axis_size(axis))
    route = [((i - distance) % len(devices), i) for i in devices]
    return lax.ppermute(block, axis, route)


def silu_slope(value):
    sig = jax.nn.sigmoid(value)
    return sig * (1.0 + value * (1.0 - sig))


def per_device(x_t, weight, cotangent, tile_row, tile_col, tile_off, tile_vals, tile_count):
    feat_rows = x_t.shape[0]
    nodes = x_t.shape[1]
    tile = tile_vals.shape[1]
    tiles = nodes // tile
    slots = tile_row.shape[0]
    span = 2 * REACH + 1
    w_cols = weight
    proj = lax.psum_scatter(
        lax.dot_general(w_cols, x_t, (((0,), (0,)), ((), ())), preferred_element_type=jnp.float32),
        "feat",
        scatter_dimension=0,
        tiled=True,
    ).astype(jnp.bfloat16)
    slab = proj.reshape(feat_rows, tiles, tile)
    fetched = {0: slab}
    for offset in range(-REACH, REACH + 1):
        if offset != 0:
            fetched[offset] = shifted(slab, "blk", -offset)
    stacked = jnp.concatenate([fetched[offset] for offset in range(-REACH, REACH + 1)], axis=1)
    live = (jnp.arange(slots, dtype=jnp.int32) < tile_count[0]).astype(jnp.float32)
    source_index = (tile_off + REACH) * tiles + tile_col
    pieces = jnp.take(stacked, source_index, axis=1)
    product = jnp.einsum("hsk,srk->hsr", pieces, tile_vals, preferred_element_type=jnp.float32)
    row_hot = (tile_row[:, None] == jnp.arange(tiles, dtype=jnp.int32)[None, :]).astype(
        jnp.float32
    ) * live[:, None]
    summed = jnp.einsum("hsr,st->htr", product, row_hot, precision=lax.Precision.HIGHEST)
    pre_t = summed.reshape(feat_rows, nodes)
    out_t = jax.nn.silu(pre_t).astype(jnp.bfloat16)
    grad_pre = (cotangent.astype(jnp.float32) * silu_slope(pre_t)).astype(jnp.bfloat16)
    grad_pieces = jnp.take(grad_pre.reshape(feat_rows, tiles, tile), tile_row, axis=1)
    contrib = jnp.einsum("hsr,srk->hsk", grad_pieces, tile_vals, preferred_element_type=jnp.float32)
    dest_hot = (source_index[:, None] == jnp.arange(span * tiles, dtype=jnp.int32)[None, :]).astype(
        jnp.float32
    ) * live[:, None]
    buffers = jnp.einsum("hsk,sd->hdk", contrib, dest_hot, precision=lax.Precision.HIGHEST)

    def bound_for(offset):
        return buffers[:, (offset + REACH) * tiles : (offset + REACH + 1) * tiles, :]

    gathered_sum = bound_for(0)
    for offset in range(-REACH, REACH + 1):
        if offset != 0:
            gathered_sum = gathered_sum + shifted(bound_for(offset), "blk", offset)
    grad_proj = gathered_sum.reshape(feat_rows, nodes).astype(jnp.bfloat16)
    piece = lax.all_gather(grad_proj, "feat", axis=0, tiled=True)
    block = lax.dot_general(
        x_t, piece, (((1,), (1,)), ((), ())), preferred_element_type=jnp.float32
    )
    weight_grad = block
    w_cols = weight
    input_grad = jnp.dot(w_cols, piece, preferred_element_type=jnp.float32)
    weight_grad, input_grad = (weight_grad, input_grad)
    factor = 1.0 / math.sqrt(nodes * lax.axis_size("blk"))
    weight_grad = lax.psum(weight_grad * factor, "blk")
    return (out_t, input_grad.astype(jnp.bfloat16), weight_grad)


def solution(mesh):
    placed = (
        P("feat", "blk"),
        P("feat", None),
        P("feat", "blk"),
        P("blk"),
        P("blk"),
        P("blk"),
        P("blk", None, None),
        P("blk"),
    )
    return jax.shard_map(
        per_device,
        mesh=mesh,
        in_specs=placed,
        out_specs=(P("feat", "blk"), P("feat", "blk"), P("feat", None)),
        check_vma=False,
    )
```

profile of v0, /device:TPU:26, one launch (start us, length us, event | category | flops | bytes accessed | tf_op | source)
XLA Modules:
  0.0 1056.2 jit_solution(13803362977749975269)
XLA Ops:
  7.3 1.0 copy-done
  8.2 3.4 fusion.58
  11.8 58.4 %reduce-scatter.2.cloned.1.call-done = f32[64,4096]{1,0:T(8,128)} async-done(((f32[256,4096]{1,0:T(8,128)}), f32[64,4096]{1,0:T(8,128)}) %reduce-scatter.2.cloned.1.call-update) | async-done | bytes 1048592 | tf_op jit(solution)/shard_map/reduce_scatter | solution.py:29
  70.2 1.4 copy_bitcast_fusion.2
  71.6 3.4 collective-permute-start.1
  75.0 2.1 collective-permute-start
  77.1 1.5 collective-permute-start.2
  79.2 0.7 collective-permute-start.3
  79.9 1.5 collective-permute-start.6
  81.4 19.7 %collective-permute-done = bf16[64,32,128]{2,0,1:T(8,128)(2,1)S(1)} collective-permute-done((bf16[64,32,128]{2,0,1:T(8,128)(2,1)S(1)}, bf16[64,32,128]{2,0,1:T(8,128)(2,1)S(1)}, u32[]{:S(2)}, u32[]{:S(2)}) %collective-permute-start) | collective-permute-done | bytes 524320 | tf_op jit(solution)/shard_map/ppermute | solution.py:13
  101.1 16.5 %collective-permute-start.5 = (bf16[64,32,128]{2,0,1:T(8,128)(2,1)S(1)}, bf16[64,32,128]{2,0,1:T(8,128)(2,1)S(1)}, u32[]{:S(2)}, u32[]{:S(2)}) collective-permute-start(bf16[64,32,128]{2,0,1:T(8,128)(2,1)S(1)} %copy_bitcast_fusion.2), channel_id=1, source_target_pairs={{8,0},{12,4},{16,8},{20,12},{24,16},{28,20},{32,24},{36,28},{40,32... | collective-permute-start | bytes 1572872 | tf_op jit(solution)/shard_map/ppermute | solution.py:13
  117.6 0.8 constant_dynamic-update-slice_fusion.8
  118.4 5.3 collective-permute-start.4
  123.7 0.8 constant_dynamic-update-slice_fusion.7
  124.6 3.6 collective-permute-start.7
  128.1 0.8 constant_dynamic-update-slice_fusion.6
  129.0 10.7 %collective-permute-done.3 = bf16[64,32,128]{2,0,1:T(8,128)(2,1)S(1)} collective-permute-done((bf16[64,32,128]{2,0,1:T(8,128)(2,1)S(1)}, bf16[64,32,128]{2,0,1:T(8,128)(2,1)S(1)}, u32[]{:S(2)}, u32[]{:S(2)}) %collective-permute-start.3) | collective-permute-done | bytes 524320 | tf_op jit(solution)/shard_map/ppermute | solution.py:13
  139.7 0.8 constant_dynamic-update-slice_fusion.5
  140.5 0.9 constant_dynamic-update-slice_fusion.4
  141.4 18.4 %collective-permute-done.4 = bf16[64,32,128]{2,0,1:T(8,128)(2,1)S(1)} collective-permute-done((bf16[64,32,128]{2,0,1:T(8,128)(2,1)S(1)}, bf16[64,32,128]{2,0,1:T(8,128)(2,1)S(1)}, u32[]{:S(2)}, u32[]{:S(2)}) %collective-permute-start.4) | collective-permute-done | bytes 524320 | tf_op jit(solution)/shard_map/ppermute | solution.py:13
  159.8 0.8 constant_dynamic-update-slice_fusion.3
  160.7 0.8 constant_dynamic-update-slice_fusion.2
  161.5 0.8 constant_dynamic-update-slice_fusion.1
  162.3 0.8 constant_dynamic-update-slice_fusion
  163.2 5.9 gather_fusion
  169.1 15.2 %fusion.16 = f32[64,288,128]{2,0,1:T(8,128)} fusion(bf16[288,128,128]{2,1,0:T(8,128)(2,1)} %param.14, bf16[288,64,128]{2,1,0:T(8,128)(2,1)} %gather_fusion, pred[288]{0:T(512)(128)(4,1)S(1)} %get-tuple-element.3), kind=kOutput, calls=%fused_computation.17 | convolution fusion | flops 606339072 | bytes 23593248 | tf_op jit(solution)/shard_map/hsk,srk->hsr/dot_general | solution.py:44
  184.3 15.2 %fusion.2 = f32[32,64,128]{2,0,1:T(8,128)S(1)} fusion(f32[64,288,128]{2,0,1:T(8,128)} %fusion.16, f32[288]{0:T(512)S(1)} %fusion.52, s32[288]{0:T(512)S(1)} %copy-done.4), kind=kOutput, calls=%fused_computation.4 | convolution fusion | flops 905988096 | bytes 10488064 | tf_op jit(solution)/shard_map/hsr,st->htr/dot_general | solution.py:48
  199.5 1.8 fusion.41
  201.3 0.1 copy.52
  201.4 13.3 %gather_fusion.1 = bf16[288,64,128]{2,1,0:T(8,128)(2,1)} fusion(bf16[64,32,128]{2,0,1:T(8,128)(2,1)S(1)} %bitcast.81, s32[1024]{0:T(1024)S(1)} %pad_clamp_fusion), kind=kCustom, calls=%fused_computation.1 | custom fusion | bytes 9438336 | tf_op jit(solution)/shard_map/jit(_take)/gather | solution.py:52
  214.7 7.0 fusion.19
  221.7 20.5 %fusion.13 = f32[64,288,128]{2,1,0:T(8,128)S(1)} fusion(f32[64,288,128]{2,0,1:T(8,128)S(1)} %fusion.19, f32[288]{0:T(512)S(1)} %fusion.52, s32[288]{0:T(512)S(1)} %get-tuple-element.4), kind=kOutput, calls=%fused_computation.16 | convolution fusion | flops 8153892864 | bytes 18876672 | tf_op jit(solution)/shard_map/hsk,sd->hdk/dot_general | solution.py:57
  242.3 1.6 fusion.57
  243.9 0.1 collective-permute-start.8
  244.0 4.4 collective-permute-start.15
  248.4 11.7 %collective-permute-start.13 = (f32[64,32,128]{2,1,0:T(8,128)S(1)}, f32[64,32,128]{2,1,0:T(8,128)S(1)}, u32[]{:S(2)}, u32[]{:S(2)}) collective-permute-start(f32[64,32,128]{2,1,0:T(8,128)S(1)} %get-tuple-element.8), channel_id=1, source_target_pairs={{248,0},{252,4},{0,8},{4,12},{8,16},{12,20},{16,24},{20,28},{24,32... | collective-permute-start | bytes 3145736 | tf_op jit(solution)/shard_map/ppermute | solution.py:13
  260.1 27.4 %collective-permute-done.8 = f32[64,32,128]{2,1,0:T(8,128)S(1)} collective-permute-done((f32[64,32,128]{2,1,0:T(8,128)S(1)}, f32[64,32,128]{2,1,0:T(8,128)S(1)}, u32[]{:S(2)}, u32[]{:S(2)}) %collective-permute-start.8) | collective-permute-done | bytes 1048608 | tf_op jit(solution)/shard_map/ppermute | solution.py:13
  287.5 11.3 %collective-permute-start.11 = (f32[64,32,128]{2,1,0:T(8,128)S(1)}, f32[64,32,128]{2,1,0:T(8,128)S(1)}, u32[]{:S(2)}, u32[]{:S(2)}) collective-permute-start(f32[64,32,128]{2,1,0:T(8,128)S(1)} %get-tuple-element.10), channel_id=1, source_target_pairs={{4,0},{8,4},{12,8},{16,12},{20,16},{24,20},{28,24},{32,28},{36,32}... | collective-permute-start | bytes 3145736 | tf_op jit(solution)/shard_map/ppermute | solution.py:13
  298.8 71.9 %collective-permute-start.10 = (f32[64,32,128]{2,1,0:T(8,128)S(1)}, f32[64,32,128]{2,1,0:T(8,128)S(1)}, u32[]{:S(2)}, u32[]{:S(2)}) collective-permute-start(f32[64,32,128]{2,1,0:T(8,128)S(1)} %get-tuple-element.11), channel_id=1, source_target_pairs={{8,0},{12,4},{16,8},{20,12},{24,16},{28,20},{32,24},{36,28},{40,32... | collective-permute-start | bytes 3145736 | tf_op jit(solution)/shard_map/ppermute | solution.py:13
  370.8 65.4 %collective-permute-done.11 = f32[64,32,128]{2,1,0:T(8,128)S(1)} collective-permute-done((f32[64,32,128]{2,1,0:T(8,128)S(1)}, f32[64,32,128]{2,1,0:T(8,128)S(1)}, u32[]{:S(2)}, u32[]{:S(2)}) %collective-permute-start.11) | collective-permute-done | bytes 1048608 | tf_op jit(solution)/shard_map/ppermute | solution.py:13
  436.2 7.8 collective-permute-done.10
  444.0 1.2 fusion.40
  445.2 1.0 copy.51
  446.2 69.3 %all-gather.2.cloned.1.call-done = bf16[256,4096]{1,0:T(8,128)(2,1)} async-done(((bf16[64,4096]{1,0:T(8,128)(2,1)}), bf16[256,4096]{1,0:T(8,128)(2,1)}) %all-gather.2.cloned.1.call-update) | async-done | bytes 2097168 | tf_op jit(solution)/shard_map/all_gather | solution.py:67
  515.5 3.0 fusion.24
  518.5 2.9 fusion.12
  521.4 526.6 %all-reduce.2.cloned.1.call-done = f32[64,256]{1,0:T(8,128)} async-done(((f32[64,256]{1,0:T(8,128)}), f32[64,256]{1,0:T(8,128)}) %all-reduce.2.cloned.1.call-update) | async-done | bytes 65552 | tf_op jit(solution)/shard_map/psum | solution.py:76
  1048.0 1.5 copy.63
  (39 shorter events, 0.3 us)
Async XLA Ops:
  7.2 1.0 copy-start
  7.2 4.6 copy-start.4
  7.2 4.6 copy-start.6
  7.2 4.6 copy-start.5
  7.2 63.0 %reduce-scatter.2.cloned.1.call-start = ((), (), s32[]{:S(2)}) async-start(), calls=%async_computation.1 | async-start | bytes 5242880 | tf_op jit(solution)/shard_map/reduce_scatter | solution.py:29
  11.7 503.8 %all-gather.2.cloned.1.call-start = ((), (), s32[]{:S(2)}) async-start(), calls=%async_computation.2 | async-start | bytes 2621440 | tf_op jit(solution)/shard_map/all_gather | solution.py:67
  70.2 70.3 %copy-start.1 = (f32[64,4096]{1,0:T(8,128)S(1)}, f32[64,4096]{1,0:T(8,128)}, u32[]{:S(2)}) copy-start(f32[64,4096]{1,0:T(8,128)} %reduce-scatter.2.cloned.1.call-done) | copy-start | bytes 3145732
  71.6 46.8 %collective-permute-start.1 = (bf16[64,32,128]{2,0,1:T(8,128)(2,1)S(1)}, bf16[64,32,128]{2,0,1:T(8,128)(2,1)S(1)}, u32[]{:S(2)}, u32[]{:S(2)}) collective-permute-start(bf16[64,32,128]{2,0,1:T(8,128)(2,1)S(1)} %copy_bitcast_fusion.2), channel_id=1, source_target_pairs={{244,0},{248,4},{252,8},{0,12},{4,16},{8,20},{12,24},{16,28},{20,3... | collective-permute-start | bytes 1572872 | tf_op jit(solution)/shard_map/ppermute | solution.py:13
  75.0 26.1 %collective-permute-start = (bf16[64,32,128]{2,0,1:T(8,128)(2,1)S(1)}, bf16[64,32,128]{2,0,1:T(8,128)(2,1)S(1)}, u32[]{:S(2)}, u32[]{:S(2)}) collective-permute-start(bf16[64,32,128]{2,0,1:T(8,128)(2,1)S(1)} %copy_bitcast_fusion.2), channel_id=1, source_target_pairs={{240,0},{244,4},{248,8},{252,12},{0,16},{4,20},{8,24},{12,28},{16,... | collective-permute-start | bytes 1572872 | tf_op jit(solution)/shard_map/ppermute | solution.py:13
  77.1 47.5 %collective-permute-start.2 = (bf16[64,32,128]{2,0,1:T(8,128)(2,1)S(1)}, bf16[64,32,128]{2,0,1:T(8,128)(2,1)S(1)}, u32[]{:S(2)}, u32[]{:S(2)}) collective-permute-start(bf16[64,32,128]{2,0,1:T(8,128)(2,1)S(1)} %copy_bitcast_fusion.2), channel_id=1, source_target_pairs={{248,0},{252,4},{0,8},{4,12},{8,16},{12,20},{16,24},{20,28},{24,32... | collective-permute-start | bytes 1572872 | tf_op jit(solution)/shard_map/ppermute | solution.py:13
  79.2 60.4 %collective-permute-start.3 = (bf16[64,32,128]{2,0,1:T(8,128)(2,1)S(1)}, bf16[64,32,128]{2,0,1:T(8,128)(2,1)S(1)}, u32[]{:S(2)}, u32[]{:S(2)}) collective-permute-start(bf16[64,32,128]{2,0,1:T(8,128)(2,1)S(1)} %copy_bitcast_fusion.2), channel_id=1, source_target_pairs={{252,0},{0,4},{4,8},{8,12},{12,16},{16,20},{20,24},{24,28},{28,32}... | collective-permute-start | bytes 1572872 | tf_op jit(solution)/shard_map/ppermute | solution.py:13
  79.9 81.6 %collective-permute-start.6 = (bf16[64,32,128]{2,0,1:T(8,128)(2,1)S(1)}, bf16[64,32,128]{2,0,1:T(8,128)(2,1)S(1)}, u32[]{:S(2)}, u32[]{:S(2)}) collective-permute-start(bf16[64,32,128]{2,0,1:T(8,128)(2,1)S(1)} %copy_bitcast_fusion.2), channel_id=1, source_target_pairs={{12,0},{16,4},{20,8},{24,12},{28,16},{32,20},{36,24},{40,28},{44,3... | collective-permute-start | bytes 1572872 | tf_op jit(solution)/shard_map/ppermute | solution.py:13
  101.1 59.6 %collective-permute-start.5 = (bf16[64,32,128]{2,0,1:T(8,128)(2,1)S(1)}, bf16[64,32,128]{2,0,1:T(8,128)(2,1)S(1)}, u32[]{:S(2)}, u32[]{:S(2)}) collective-permute-start(bf16[64,32,128]{2,0,1:T(8,128)(2,1)S(1)} %copy_bitcast_fusion.2), channel_id=1, source_target_pairs={{8,0},{12,4},{16,8},{20,12},{24,16},{28,20},{32,24},{36,28},{40,32... | collective-permute-start | bytes 1572872 | tf_op jit(solution)/shard_map/ppermute | solution.py:13
  118.4 41.4 %collective-permute-start.4 = (bf16[64,32,128]{2,0,1:T(8,128)(2,1)S(1)}, bf16[64,32,128]{2,0,1:T(8,128)(2,1)S(1)}, u32[]{:S(2)}, u32[]{:S(2)}) collective-permute-start(bf16[64,32,128]{2,0,1:T(8,128)(2,1)S(1)} %copy_bitcast_fusion.2), channel_id=1, source_target_pairs={{4,0},{8,4},{12,8},{16,12},{20,16},{24,20},{28,24},{32,28},{36,32}... | collective-permute-start | bytes 1572872 | tf_op jit(solution)/shard_map/ppermute | solution.py:13
  124.6 37.8 %collective-permute-start.7 = (bf16[64,32,128]{2,0,1:T(8,128)(2,1)S(1)}, bf16[64,32,128]{2,0,1:T(8,128)(2,1)S(1)}, u32[]{:S(2)}, u32[]{:S(2)}) collective-permute-start(bf16[64,32,128]{2,0,1:T(8,128)(2,1)S(1)} %copy_bitcast_fusion.2), channel_id=1, source_target_pairs={{16,0},{20,4},{24,8},{28,12},{32,16},{36,20},{40,24},{44,28},{48,3... | collective-permute-start | bytes 1572872 | tf_op jit(solution)/shard_map/ppermute | solution.py:13
  184.3 15.2 %copy-start.2 = (bf16[64,4096]{1,0:T(8,128)(2,1)S(1)}, bf16[64,4096]{1,0:T(8,128)(2,1)}, u32[]{:S(2)}) copy-start(bf16[64,4096]{1,0:T(8,128)(2,1)} %param.10) | copy-start | bytes 1572868
  243.9 43.6 %collective-permute-start.8 = (f32[64,32,128]{2,1,0:T(8,128)S(1)}, f32[64,32,128]{2,1,0:T(8,128)S(1)}, u32[]{:S(2)}, u32[]{:S(2)}) collective-permute-start(f32[64,32,128]{2,1,0:T(8,128)S(1)} %get-tuple-element.5), channel_id=1, source_target_pairs={{16,0},{20,4},{24,8},{28,12},{32,16},{36,20},{40,24},{44,28},{48,3... | collective-permute-start | bytes 3145736 | tf_op jit(solution)/shard_map/ppermute | solution.py:13
  244.0 54.9 %collective-permute-start.15 = (f32[64,32,128]{2,1,0:T(8,128)S(1)}, f32[64,32,128]{2,1,0:T(8,128)S(1)}, u32[]{:S(2)}, u32[]{:S(2)}) collective-permute-start(f32[64,32,128]{2,1,0:T(8,128)S(1)} %get-tuple-element.6), channel_id=1, source_target_pairs={{240,0},{244,4},{248,8},{252,12},{0,16},{4,20},{8,24},{12,28},{16,... | collective-permute-start | bytes 3145736 | tf_op jit(solution)/shard_map/ppermute | solution.py:13
  248.4 122.4 %collective-permute-start.14 = (f32[64,32,128]{2,1,0:T(8,128)S(1)}, f32[64,32,128]{2,1,0:T(8,128)S(1)}, u32[]{:S(2)}, u32[]{:S(2)}) collective-permute-start(f32[64,32,128]{2,1,0:T(8,128)S(1)} %get-tuple-element.7), channel_id=1, source_target_pairs={{244,0},{248,4},{252,8},{0,12},{4,16},{8,20},{12,24},{16,28},{20,3... | collective-permute-start | bytes 3145736 | tf_op jit(solution)/shard_map/ppermute | solution.py:13
  248.4 122.4 %collective-permute-start.13 = (f32[64,32,128]{2,1,0:T(8,128)S(1)}, f32[64,32,128]{2,1,0:T(8,128)S(1)}, u32[]{:S(2)}, u32[]{:S(2)}) collective-permute-start(f32[64,32,128]{2,1,0:T(8,128)S(1)} %get-tuple-element.8), channel_id=1, source_target_pairs={{248,0},{252,4},{0,8},{4,12},{8,16},{12,20},{16,24},{20,28},{24,32... | collective-permute-start | bytes 3145736 | tf_op jit(solution)/shard_map/ppermute | solution.py:13
  260.1 110.7 %collective-permute-start.12 = (f32[64,32,128]{2,1,0:T(8,128)S(1)}, f32[64,32,128]{2,1,0:T(8,128)S(1)}, u32[]{:S(2)}, u32[]{:S(2)}) collective-permute-start(f32[64,32,128]{2,1,0:T(8,128)S(1)} %get-tuple-element.9), channel_id=1, source_target_pairs={{252,0},{0,4},{4,8},{8,12},{12,16},{16,20},{20,24},{24,28},{28,32}... | collective-permute-start | bytes 3145736 | tf_op jit(solution)/shard_map/ppermute | solution.py:13
  287.5 148.7 %collective-permute-start.11 = (f32[64,32,128]{2,1,0:T(8,128)S(1)}, f32[64,32,128]{2,1,0:T(8,128)S(1)}, u32[]{:S(2)}, u32[]{:S(2)}) collective-permute-start(f32[64,32,128]{2,1,0:T(8,128)S(1)} %get-tuple-element.10), channel_id=1, source_target_pairs={{4,0},{8,4},{12,8},{16,12},{20,16},{24,20},{28,24},{32,28},{36,32}... | collective-permute-start | bytes 3145736 | tf_op jit(solution)/shard_map/ppermute | solution.py:13
  298.8 145.2 %collective-permute-start.10 = (f32[64,32,128]{2,1,0:T(8,128)S(1)}, f32[64,32,128]{2,1,0:T(8,128)S(1)}, u32[]{:S(2)}, u32[]{:S(2)}) collective-permute-start(f32[64,32,128]{2,1,0:T(8,128)S(1)} %get-tuple-element.11), channel_id=1, source_target_pairs={{8,0},{12,4},{16,8},{20,12},{24,16},{28,20},{32,24},{36,28},{40,32... | collective-permute-start | bytes 3145736 | tf_op jit(solution)/shard_map/ppermute | solution.py:13
  370.8 147.8 %copy-start.3 = (bf16[64,256]{1,0:T(8,128)(2,1)S(1)}, bf16[64,256]{1,0:T(8,128)(2,1)}, u32[]{:S(2)}) copy-start(bf16[64,256]{1,0:T(8,128)(2,1)} %param.9) | copy-start | bytes 98308
  370.8 73.2 %collective-permute-start.9 = (f32[64,32,128]{2,1,0:T(8,128)S(1)}, f32[64,32,128]{2,1,0:T(8,128)S(1)}, u32[]{:S(2)}, u32[]{:S(2)}) collective-permute-start(f32[64,32,128]{2,1,0:T(8,128)S(1)} %get-tuple-element.12), channel_id=1, source_target_pairs={{12,0},{16,4},{20,8},{24,12},{28,16},{32,20},{36,24},{40,28},{44,3... | collective-permute-start | bytes 3145736 | tf_op jit(solution)/shard_map/ppermute | solution.py:13
  446.2 601.8 %all-reduce.2.cloned.1.call-start = ((), (), s32[]{:S(2)}) async-start(), calls=%async_computation.3 | async-start | bytes 131072 | tf_op jit(solution)/shard_map/psum | solution.py:76
Sparse Core Ops, SparseCore 0:
  11.8 58.3 reduce-scatter.1
  446.3 69.1 all-gather.1
  518.9 529.0 all-reduce.1
where the time goes:
time: 1060 us
  waiting for transfers between devices  804 us (76%)
  starting transfers between devices  134 us (13%)
  matrix products  67.2 us (6%)
  local copies, waits for them, and re-layouts  31.1 us (3%)
  between operations  14.8 us (1%)
    psum x1, waiting for transfers between devices, per_device(): weight_grad = lax.psum(weight_grad * factor, 'blk')  527 us
    ppermute x16, waiting for transfers between devices, shifted(): return lax.ppermute(block, axis, route)  149 us
    ppermute x16, starting transfers between devices, shifted(): return lax.ppermute(block, axis, route)  134 us
    all_gather x1, waiting for transfers between devices, per_device(): piece = lax.all_gather(grad_proj, 'feat', axis=0, tiled=True)  69.3 us
    reduce_scatter x1, waiting for transfers between devices, per_device(): lax.psum_scatter(lax.dot_general(w_cols, x_t, (((0,), (0,)), ((), ())), p...  58.4 us
  transfers between devices with their start and end apart: 19, of which 9 were waited for; matrix products, arithmetic and copies ran while one was open for 1% of the time, Pallas kernels for 0%

commit v1 on v0

--- a/solution.py
+++ b/solution.py
@@ -73,7 +73,7 @@
     input_grad = jnp.dot(w_cols, piece, preferred_element_type=jnp.float32)
     weight_grad, input_grad = (weight_grad, input_grad)
     factor = 1.0 / math.sqrt(nodes * lax.axis_size("blk"))
-    weight_grad = lax.psum(weight_grad * factor, "blk")
+    weight_grad = jnp.sum(lax.all_gather(weight_grad * factor, "blk"), axis=0)
     return (out_t, input_grad.astype(jnp.bfloat16), weight_grad)
 
 

time: 1060 us -> 839 us (0.79)
  the two profiles are of different devices: /device:TPU:26 before, /device:TPU:4 now
where the time goes in v1:
time: 839 us; the launch traced here: 834 us
  waiting for transfers between devices  672 us (80%)
  matrix products  67.2 us (8%)
  starting transfers between devices  41.1 us (5%)
  local copies, waits for them, and re-layouts  29.6 us (4%)
  between operations  14.9 us (2%)
  other arithmetic  8.39 us (1%)
    all_gather x1, waiting for transfers between devices, per_device(): weight_grad = jnp.sum(lax.all_gather(weight_grad * factor, 'blk'), axis=0)  304 us
    ppermute x16, waiting for transfers between devices, shifted(): return lax.ppermute(block, axis, route)  286 us
    reduce_scatter x1, waiting for transfers between devices, per_device(): lax.psum_scatter(lax.dot_general(w_cols, x_t, (((0,), (0,)), ((), ())), p...  56.9 us
    ppermute x16, starting transfers between devices, shifted(): return lax.ppermute(block, axis, route)  41 us
    all_gather x1, waiting for transfers between devices, per_device(): piece = lax.all_gather(grad_proj, 'feat', axis=0, tiled=True)  25.8 us
    dot_general x1, matrix products, per_device(): jnp.einsum('hsk,sd->hdk', contrib, dest_hot, precision=lax.Precision.HIGH...  20.5 us
  transfers between devices with their start and end apart: 19, of which 12 were waited for; matrix products, arithmetic and copies ran while one was open for 1% of the time, Pallas kernels for 0%

profile of v1, /device:TPU:4, one launch (start us, length us, event | category | flops | bytes accessed | tf_op | source)
XLA Modules:
  0.0 833.6 jit_solution(6405699857895598452)
XLA Ops:
  7.3 1.0 copy-done
  8.2 3.4 fusion.58
  11.8 56.9 %reduce-scatter.2.cloned.1.call-done = f32[64,4096]{1,0:T(8,128)} async-done(((f32[256,4096]{1,0:T(8,128)}), f32[64,4096]{1,0:T(8,128)}) %reduce-scatter.2.cloned.1.call-update) | async-done | bytes 1048592 | tf_op jit(solution)/shard_map/reduce_scatter | solution.py:29
  68.7 1.4 copy_bitcast_fusion.2
  70.1 3.3 collective-permute-start.1
  73.4 2.7 collective-permute-start
  76.1 0.9 collective-permute-start.2
  77.7 0.9 collective-permute-start.3
  78.6 6.0 collective-permute-start.6
  84.7 26.6 %collective-permute-done = bf16[64,32,128]{2,0,1:T(8,128)(2,1)S(1)} collective-permute-done((bf16[64,32,128]{2,0,1:T(8,128)(2,1)S(1)}, bf16[64,32,128]{2,0,1:T(8,128)(2,1)S(1)}, u32[]{:S(2)}, u32[]{:S(2)}) %collective-permute-start) | collective-permute-done | bytes 524320 | tf_op jit(solution)/shard_map/ppermute | solution.py:13
  111.3 14.4 %collective-permute-start.5 = (bf16[64,32,128]{2,0,1:T(8,128)(2,1)S(1)}, bf16[64,32,128]{2,0,1:T(8,128)(2,1)S(1)}, u32[]{:S(2)}, u32[]{:S(2)}) collective-permute-start(bf16[64,32,128]{2,0,1:T(8,128)(2,1)S(1)} %copy_bitcast_fusion.2), channel_id=1, source_target_pairs={{8,0},{12,4},{16,8},{20,12},{24,16},{28,20},{32,24},{36,28},{40,32... | collective-permute-start | bytes 1572872 | tf_op jit(solution)/shard_map/ppermute | solution.py:13
  125.6 0.8 constant_dynamic-update-slice_fusion.8
  126.5 0.9 constant_dynamic-update-slice_fusion.7
  127.3 0.2 collective-permute-start.7
  127.5 0.8 constant_dynamic-update-slice_fusion.6
  128.3 6.6 collective-permute-done.3
  134.9 0.8 constant_dynamic-update-slice_fusion.5
  135.7 0.9 constant_dynamic-update-slice_fusion.4
  136.7 19.0 %collective-permute-done.4 = bf16[64,32,128]{2,0,1:T(8,128)(2,1)S(1)} collective-permute-done((bf16[64,32,128]{2,0,1:T(8,128)(2,1)S(1)}, bf16[64,32,128]{2,0,1:T(8,128)(2,1)S(1)}, u32[]{:S(2)}, u32[]{:S(2)}) %collective-permute-start.4) | collective-permute-done | bytes 524320 | tf_op jit(solution)/shard_map/ppermute | solution.py:13
  155.7 0.8 constant_dynamic-update-slice_fusion.3
  156.5 0.8 constant_dynamic-update-slice_fusion.2
  157.4 0.8 constant_dynamic-update-slice_fusion.1
  158.2 7.8 collective-permute-done.7
  166.0 0.8 constant_dynamic-update-slice_fusion
  166.9 5.9 gather_fusion
  172.7 15.2 %fusion.16 = f32[64,288,128]{2,0,1:T(8,128)} fusion(bf16[288,128,128]{2,1,0:T(8,128)(2,1)} %param.14, bf16[288,64,128]{2,1,0:T(8,128)(2,1)} %gather_fusion, pred[288]{0:T(512)(128)(4,1)S(1)} %get-tuple-element.3), kind=kOutput, calls=%fused_computation.17 | convolution fusion | flops 606339072 | bytes 23593248 | tf_op jit(solution)/shard_map/hsk,srk->hsr/dot_general | solution.py:44
  187.9 15.2 %fusion.2 = f32[32,64,128]{2,0,1:T(8,128)S(1)} fusion(f32[64,288,128]{2,0,1:T(8,128)} %fusion.16, f32[288]{0:T(512)S(1)} %fusion.52, s32[288]{0:T(512)S(1)} %copy-done.4), kind=kOutput, calls=%fused_computation.4 | convolution fusion | flops 905988096 | bytes 10488064 | tf_op jit(solution)/shard_map/hsr,st->htr/dot_general | solution.py:48
  203.2 1.8 fusion.41
  205.1 13.3 %gather_fusion.1 = bf16[288,64,128]{2,1,0:T(8,128)(2,1)} fusion(bf16[64,32,128]{2,0,1:T(8,128)(2,1)S(1)} %bitcast.82, s32[1024]{0:T(1024)S(1)} %pad_clamp_fusion), kind=kCustom, calls=%fused_computation.1 | custom fusion | bytes 9438336 | tf_op jit(solution)/shard_map/jit(_take)/gather | solution.py:52
  218.4 7.0 fusion.19
  225.4 20.5 %fusion.13 = f32[64,288,128]{2,1,0:T(8,128)S(1)} fusion(f32[64,288,128]{2,0,1:T(8,128)S(1)} %fusion.19, f32[288]{0:T(512)S(1)} %fusion.52, s32[288]{0:T(512)S(1)} %get-tuple-element.4), kind=kOutput, calls=%fused_computation.16 | convolution fusion | flops 8153892864 | bytes 18876672 | tf_op jit(solution)/shard_map/hsk,sd->hdk/dot_general | solution.py:57
  246.0 1.6 fusion.57
  247.5 6.2 collective-permute-start.8
  253.7 0.2 collective-permute-start.15
  253.9 5.8 collective-permute-start.12
  259.7 112.2 %collective-permute-done.8 = f32[64,32,128]{2,1,0:T(8,128)S(1)} collective-permute-done((f32[64,32,128]{2,1,0:T(8,128)S(1)}, f32[64,32,128]{2,1,0:T(8,128)S(1)}, u32[]{:S(2)}, u32[]{:S(2)}) %collective-permute-start.8) | collective-permute-done | bytes 1048608 | tf_op jit(solution)/shard_map/ppermute | solution.py:13
  371.9 0.2 collective-permute-start.11
  372.3 6.2 collective-permute-done.13
  378.6 54.1 %collective-permute-done.11 = f32[64,32,128]{2,1,0:T(8,128)S(1)} collective-permute-done((f32[64,32,128]{2,1,0:T(8,128)S(1)}, f32[64,32,128]{2,1,0:T(8,128)S(1)}, u32[]{:S(2)}, u32[]{:S(2)}) %collective-permute-start.11) | collective-permute-done | bytes 1048608 | tf_op jit(solution)/shard_map/ppermute | solution.py:13
  432.7 34.5 %collective-permute-done.10 = f32[64,32,128]{2,1,0:T(8,128)S(1)} collective-permute-done((f32[64,32,128]{2,1,0:T(8,128)S(1)}, f32[64,32,128]{2,1,0:T(8,128)S(1)}, u32[]{:S(2)}, u32[]{:S(2)}) %collective-permute-start.10) | collective-permute-done | bytes 1048608 | tf_op jit(solution)/shard_map/ppermute | solution.py:13
  467.2 18.8 %collective-permute-done.9 = f32[64,32,128]{2,1,0:T(8,128)S(1)} collective-permute-done((f32[64,32,128]{2,1,0:T(8,128)S(1)}, f32[64,32,128]{2,1,0:T(8,128)S(1)}, u32[]{:S(2)}, u32[]{:S(2)}) %collective-permute-start.9) | collective-permute-done | bytes 1048608 | tf_op jit(solution)/shard_map/ppermute | solution.py:13
  486.0 1.2 fusion.40
  487.1 1.0 copy.51
  488.2 25.8 %all-gather.4.cloned.1.call-done = bf16[256,4096]{1,0:T(8,128)(2,1)} async-done(((bf16[64,4096]{1,0:T(8,128)(2,1)}), bf16[256,4096]{1,0:T(8,128)(2,1)}) %all-gather.4.cloned.1.call-update) | async-done | bytes 2097168 | tf_op jit(solution)/shard_map/all_gather | solution.py:67
  514.0 3.0 fusion.24
  517.0 2.9 fusion.12
  519.9 303.8 %all-gather.6.cloned.1.call-done = f32[4096,256]{1,0:T(8,128)} async-done(((f32[64,256]{1,0:T(8,128)}), f32[4096,256]{1,0:T(8,128)}) %all-gather.6.cloned.1.call-update) | async-done | bytes 4194320 | tf_op jit(solution)/shard_map/all_gather | solution.py:76
  823.7 3.1 reduce_sum.9
  (39 shorter events, 0.6 us)
Async XLA Ops:
  7.2 1.0 copy-start
  7.2 4.6 copy-start.4
  7.2 4.6 copy-start.6
  7.2 4.6 copy-start.5
  7.2 61.5 %reduce-scatter.2.cloned.1.call-start = ((), (), s32[]{:S(2)}) async-start(), calls=%async_computation.1 | async-start | bytes 5242880 | tf_op jit(solution)/shard_map/reduce_scatter | solution.py:29
  11.7 502.3 %all-gather.4.cloned.1.call-start = ((), (), s32[]{:S(2)}) async-start(), calls=%async_computation.2 | async-start | bytes 2621440 | tf_op jit(solution)/shard_map/all_gather | solution.py:67
  68.7 67.1 %copy-start.1 = (f32[64,4096]{1,0:T(8,128)S(1)}, f32[64,4096]{1,0:T(8,128)}, u32[]{:S(2)}) copy-start(f32[64,4096]{1,0:T(8,128)} %reduce-scatter.2.cloned.1.call-done) | copy-start | bytes 3145732
  70.1 56.4 %collective-permute-start.1 = (bf16[64,32,128]{2,0,1:T(8,128)(2,1)S(1)}, bf16[64,32,128]{2,0,1:T(8,128)(2,1)S(1)}, u32[]{:S(2)}, u32[]{:S(2)}) collective-permute-start(bf16[64,32,128]{2,0,1:T(8,128)(2,1)S(1)} %copy_bitcast_fusion.2), channel_id=1, source_target_pairs={{244,0},{248,4},{252,8},{0,12},{4,16},{8,20},{12,24},{16,28},{20,3... | collective-permute-start | bytes 1572872 | tf_op jit(solution)/shard_map/ppermute | solution.py:13
  73.4 37.8 %collective-permute-start = (bf16[64,32,128]{2,0,1:T(8,128)(2,1)S(1)}, bf16[64,32,128]{2,0,1:T(8,128)(2,1)S(1)}, u32[]{:S(2)}, u32[]{:S(2)}) collective-permute-start(bf16[64,32,128]{2,0,1:T(8,128)(2,1)S(1)} %copy_bitcast_fusion.2), channel_id=1, source_target_pairs={{240,0},{244,4},{248,8},{252,12},{0,16},{4,20},{8,24},{12,28},{16,... | collective-permute-start | bytes 1572872 | tf_op jit(solution)/shard_map/ppermute | solution.py:13
  76.1 51.2 %collective-permute-start.2 = (bf16[64,32,128]{2,0,1:T(8,128)(2,1)S(1)}, bf16[64,32,128]{2,0,1:T(8,128)(2,1)S(1)}, u32[]{:S(2)}, u32[]{:S(2)}) collective-permute-start(bf16[64,32,128]{2,0,1:T(8,128)(2,1)S(1)} %copy_bitcast_fusion.2), channel_id=1, source_target_pairs={{248,0},{252,4},{0,8},{4,12},{8,16},{12,20},{16,24},{20,28},{24,32... | collective-permute-start | bytes 1572872 | tf_op jit(solution)/shard_map/ppermute | solution.py:13
  77.7 57.2 %collective-permute-start.3 = (bf16[64,32,128]{2,0,1:T(8,128)(2,1)S(1)}, bf16[64,32,128]{2,0,1:T(8,128)(2,1)S(1)}, u32[]{:S(2)}, u32[]{:S(2)}) collective-permute-start(bf16[64,32,128]{2,0,1:T(8,128)(2,1)S(1)} %copy_bitcast_fusion.2), channel_id=1, source_target_pairs={{252,0},{0,4},{4,8},{8,12},{12,16},{16,20},{20,24},{24,28},{28,32}... | collective-permute-start | bytes 1572872 | tf_op jit(solution)/shard_map/ppermute | solution.py:13
  78.6 78.8 %collective-permute-start.6 = (bf16[64,32,128]{2,0,1:T(8,128)(2,1)S(1)}, bf16[64,32,128]{2,0,1:T(8,128)(2,1)S(1)}, u32[]{:S(2)}, u32[]{:S(2)}) collective-permute-start(bf16[64,32,128]{2,0,1:T(8,128)(2,1)S(1)} %copy_bitcast_fusion.2), channel_id=1, source_target_pairs={{12,0},{16,4},{20,8},{24,12},{28,16},{32,20},{36,24},{40,28},{44,3... | collective-permute-start | bytes 1572872 | tf_op jit(solution)/shard_map/ppermute | solution.py:13
  111.3 45.3 %collective-permute-start.5 = (bf16[64,32,128]{2,0,1:T(8,128)(2,1)S(1)}, bf16[64,32,128]{2,0,1:T(8,128)(2,1)S(1)}, u32[]{:S(2)}, u32[]{:S(2)}) collective-permute-start(bf16[64,32,128]{2,0,1:T(8,128)(2,1)S(1)} %copy_bitcast_fusion.2), channel_id=1, source_target_pairs={{8,0},{12,4},{16,8},{20,12},{24,16},{28,20},{32,24},{36,28},{40,32... | collective-permute-start | bytes 1572872 | tf_op jit(solution)/shard_map/ppermute | solution.py:13
  126.5 29.2 %collective-permute-start.4 = (bf16[64,32,128]{2,0,1:T(8,128)(2,1)S(1)}, bf16[64,32,128]{2,0,1:T(8,128)(2,1)S(1)}, u32[]{:S(2)}, u32[]{:S(2)}) collective-permute-start(bf16[64,32,128]{2,0,1:T(8,128)(2,1)S(1)} %copy_bitcast_fusion.2), channel_id=1, source_target_pairs={{4,0},{8,4},{12,8},{16,12},{20,16},{24,20},{28,24},{32,28},{36,32}... | collective-permute-start | bytes 1572872 | tf_op jit(solution)/shard_map/ppermute | solution.py:13
  127.3 38.7 %collective-permute-start.7 = (bf16[64,32,128]{2,0,1:T(8,128)(2,1)S(1)}, bf16[64,32,128]{2,0,1:T(8,128)(2,1)S(1)}, u32[]{:S(2)}, u32[]{:S(2)}) collective-permute-start(bf16[64,32,128]{2,0,1:T(8,128)(2,1)S(1)} %copy_bitcast_fusion.2), channel_id=1, source_target_pairs={{16,0},{20,4},{24,8},{28,12},{32,16},{36,20},{40,24},{44,28},{48,3... | collective-permute-start | bytes 1572872 | tf_op jit(solution)/shard_map/ppermute | solution.py:13
  187.9 15.2 %copy-start.2 = (bf16[64,4096]{1,0:T(8,128)(2,1)S(1)}, bf16[64,4096]{1,0:T(8,128)(2,1)}, u32[]{:S(2)}) copy-start(bf16[64,4096]{1,0:T(8,128)(2,1)} %param.10) | copy-start | bytes 1572868
  247.5 124.4 %collective-permute-start.8 = (f32[64,32,128]{2,1,0:T(8,128)S(1)}, f32[64,32,128]{2,1,0:T(8,128)S(1)}, u32[]{:S(2)}, u32[]{:S(2)}) collective-permute-start(f32[64,32,128]{2,1,0:T(8,128)S(1)} %get-tuple-element.5), channel_id=1, source_target_pairs={{16,0},{20,4},{24,8},{28,12},{32,16},{36,20},{40,24},{44,28},{48,3... | collective-permute-start | bytes 3145736 | tf_op jit(solution)/shard_map/ppermute | solution.py:13
  253.7 118.4 %collective-permute-start.15 = (f32[64,32,128]{2,1,0:T(8,128)S(1)}, f32[64,32,128]{2,1,0:T(8,128)S(1)}, u32[]{:S(2)}, u32[]{:S(2)}) collective-permute-start(f32[64,32,128]{2,1,0:T(8,128)S(1)} %get-tuple-element.6), channel_id=1, source_target_pairs={{240,0},{244,4},{248,8},{252,12},{0,16},{4,20},{8,24},{12,28},{16,... | collective-permute-start | bytes 3145736 | tf_op jit(solution)/shard_map/ppermute | solution.py:13
  253.9 118.3 %collective-permute-start.14 = (f32[64,32,128]{2,1,0:T(8,128)S(1)}, f32[64,32,128]{2,1,0:T(8,128)S(1)}, u32[]{:S(2)}, u32[]{:S(2)}) collective-permute-start(f32[64,32,128]{2,1,0:T(8,128)S(1)} %get-tuple-element.7), channel_id=1, source_target_pairs={{244,0},{248,4},{252,8},{0,12},{4,16},{8,20},{12,24},{16,28},{20,3... | collective-permute-start | bytes 3145736 | tf_op jit(solution)/shard_map/ppermute | solution.py:13
  253.9 124.7 %collective-permute-start.13 = (f32[64,32,128]{2,1,0:T(8,128)S(1)}, f32[64,32,128]{2,1,0:T(8,128)S(1)}, u32[]{:S(2)}, u32[]{:S(2)}) collective-permute-start(f32[64,32,128]{2,1,0:T(8,128)S(1)} %get-tuple-element.8), channel_id=1, source_target_pairs={{248,0},{252,4},{0,8},{4,12},{8,16},{12,20},{16,24},{20,28},{24,32... | collective-permute-start | bytes 3145736 | tf_op jit(solution)/shard_map/ppermute | solution.py:13
  253.9 124.7 %collective-permute-start.12 = (f32[64,32,128]{2,1,0:T(8,128)S(1)}, f32[64,32,128]{2,1,0:T(8,128)S(1)}, u32[]{:S(2)}, u32[]{:S(2)}) collective-permute-start(f32[64,32,128]{2,1,0:T(8,128)S(1)} %get-tuple-element.9), channel_id=1, source_target_pairs={{252,0},{0,4},{4,8},{8,12},{12,16},{16,20},{20,24},{24,28},{28,32}... | collective-permute-start | bytes 3145736 | tf_op jit(solution)/shard_map/ppermute | solution.py:13
  371.9 60.8 %collective-permute-start.11 = (f32[64,32,128]{2,1,0:T(8,128)S(1)}, f32[64,32,128]{2,1,0:T(8,128)S(1)}, u32[]{:S(2)}, u32[]{:S(2)}) collective-permute-start(f32[64,32,128]{2,1,0:T(8,128)S(1)} %get-tuple-element.10), channel_id=1, source_target_pairs={{4,0},{8,4},{12,8},{16,12},{20,16},{24,20},{28,24},{32,28},{36,32}... | collective-permute-start | bytes 3145736 | tf_op jit(solution)/shard_map/ppermute | solution.py:13
  372.1 95.0 %collective-permute-start.10 = (f32[64,32,128]{2,1,0:T(8,128)S(1)}, f32[64,32,128]{2,1,0:T(8,128)S(1)}, u32[]{:S(2)}, u32[]{:S(2)}) collective-permute-start(f32[64,32,128]{2,1,0:T(8,128)S(1)} %get-tuple-element.11), channel_id=1, source_target_pairs={{8,0},{12,4},{16,8},{20,12},{24,16},{28,20},{32,24},{36,28},{40,32... | collective-permute-start | bytes 3145736 | tf_op jit(solution)/shard_map/ppermute | solution.py:13
  372.2 144.8 %copy-start.3 = (bf16[64,256]{1,0:T(8,128)(2,1)S(1)}, bf16[64,256]{1,0:T(8,128)(2,1)}, u32[]{:S(2)}) copy-start(bf16[64,256]{1,0:T(8,128)(2,1)} %param.9) | copy-start | bytes 98308
  372.3 113.7 %collective-permute-start.9 = (f32[64,32,128]{2,1,0:T(8,128)S(1)}, f32[64,32,128]{2,1,0:T(8,128)S(1)}, u32[]{:S(2)}, u32[]{:S(2)}) collective-permute-start(f32[64,32,128]{2,1,0:T(8,128)S(1)} %get-tuple-element.12), channel_id=1, source_target_pairs={{12,0},{16,4},{20,8},{24,12},{28,16},{32,20},{36,24},{40,28},{44,3... | collective-permute-start | bytes 3145736 | tf_op jit(solution)/shard_map/ppermute | solution.py:13
  488.1 335.6 %all-gather.6.cloned.1.call-start = ((), (), s32[]{:S(2)}) async-start(), calls=%async_computation.3 | async-start | bytes 4259840 | tf_op jit(solution)/shard_map/all_gather | solution.py:76
Sparse Core Ops, SparseCore 0:
  11.8 56.8 reduce-scatter.1
  488.3 25.6 all-gather.3
  517.1 306.5 all-gather.5
